TPU v7x, 256 devices: a whole 4x4x8 slice. The times are simulated.
256 devices in a mesh: hb: 4 (over y), row: 16 (over z, x_hi), col: 4 (over x_lo, core).
Axes of the slice: x: 4 (x_hi: 2, x_lo: 2; x = x_hi * 2 + x_lo), y: 4, z: 8, core: 2. Of those that a mesh axis runs over, the one named last changes fastest.
Arguments:
- cell_state: float32 [256, 8, 256, 512], P('hb', None, 'row', 'col'), may hold values from -6 to 6
- normalizer: float32 [256, 8, 256], P('hb', None, 'row'), may hold values from 0.1 to 4
- stabilizer: float32 [256, 8, 16], P('hb', None, 'row'), may hold values from -5 to 120
- queries: float32 [256, 8, 256], P('hb', None, 'row'), may hold values from 0.0125 to 0.1125
- key_vectors: float32 [256, 8, 256], P('hb', None, 'row'), may hold values from -6 to 6
- token_value_vectors: float32 [256, 8, 512], P('hb', None, 'col'), may hold values from -6 to 6
- input_gate: float32 [256, 8], P('hb'), may hold values from -3 to 3
- forget_gate: float32 [256, 8], P('hb'), may hold values from -1 to 5
- output_gate_logits: float32 [256, 8, 512], P('hb', None, 'col'), may hold values from -6 to 6
- norm_gain: float32 [8, 512], P(None, 'col'), may hold values from 0.5 to 1.5
- out_weight: bfloat16 [8, 512, 4096], P('hb', 'col', 'row'), may hold values from -0.09375 to 0.09375
Outputs:
- layer_out: float32 [256, 4096], P('hb', 'row')
- readout: float32 [256, 8, 512], P('hb', None, 'col')
- refreshed_cell: float32 [256, 8, 256, 512], P('hb', None, 'row', 'col')
- new_normal: float32 [256, 8, 256], P('hb', None, 'row')
- new_stab: float32 [256, 8, 16], P('hb', None, 'row')
All inputs are finite; a program needn't handle non-finite values.
Results may differ from a plain program's by a relative error of at most 0.0029.
Values may be sent and summed in bfloat16 or wider, within the bound.
No kernel may reach another device: no remote copies, remote signals or barrier semaphores. Data moves between devices by JAX's collectives and lax.ppermute only.
A program may use at most 64 MiB of HBM per device.

v0:
```python
import jax
import jax.numpy as jnp
from jax import lax
from jax.sharding import Mesh
from jax.sharding import PartitionSpec as P

DK = 256
DV = 512
RBLK = 16
ROW = ("row_0", "row_1")


def all_in_one(x, axis):
    leaves = jax.tree.leaves(x)
    order = sorted(range(len(leaves)), key=lambda k: -leaves[k].size)
    width = (1, *leaves[order[0]].shape)[-1]
    lines = [
        jnp.pad(leaves[k].reshape(-1), (0, -leaves[k].size % width)).reshape(-1, width)
        for k in order
    ]
    both, at, found = (lax.all_gather(jnp.concatenate(lines), axis), 0, {})
    for k, line in zip(order, lines):
        share = both[:, at : at + len(line)].reshape(len(both), -1)
        found[k] = share[:, : leaves[k].size].reshape(-1, *leaves[k].shape)
        at += len(line)
    numbers = iter(range(len(leaves)))
    return jax.tree.map(lambda _: found[next(numbers)], x)


def combined_by_axis(x, axes, combine):
    for axis in axes:
        pieces = all_in_one(x, axis)
        x = jax.tree.map(lambda part: part[0], pieces)
        for k in range(1, lax.axis_size(axis)):
            x = combine(x, jax.tree.map(lambda part: part[k], pieces))
    return x


def sent_to_all(x, axis):
    copies = jnp.broadcast_to(x, (lax.axis_size(axis), *x.shape))
    return lax.all_to_all(copies, axis, split_axis=0, concat_axis=0, tiled=True)


def over_copies(x, axis):
    everything = sent_to_all(x, axis)
    return jnp.sum(everything, axis=0)


def together(arrays, axis):
    ends = [0]
    for a in arrays:
        ends.append(ends[-1] + a.size)
    running = over_copies(jnp.concatenate([a.ravel() for a in arrays]), axis)
    return tuple((running[b:e].reshape(a.shape) for a, b, e in zip(arrays, ends, ends[1:])))


def combine_pairs(left_pair, right_pair):
    joined = jnp.maximum(left_pair[0], right_pair[0])
    left_scale = jnp.exp(left_pair[0] - joined)
    right_scale = jnp.exp(right_pair[0] - joined)
    numerator = left_pair[1] * left_scale[:, :, None] + right_pair[1] * right_scale[:, :, None]
    denom = left_pair[2] * left_scale + right_pair[2] * right_scale
    return (joined, numerator, denom)


def local(
    cell_state,
    normalizer,
    stabilizer,
    queries,
    key_vectors,
    token_value_vectors,
    input_gate,
    forget_gate,
    output_gate_logits,
    norm_gain,
    out_weight,
):
    carried = jax.nn.log_sigmoid(forget_gate)[:, :, None] + stabilizer
    fresh = jnp.maximum(carried, input_gate[:, :, None])
    keep = jnp.repeat(jnp.exp(carried - fresh), RBLK, axis=2)
    admit = jnp.repeat(jnp.exp(input_gate[:, :, None] - fresh), RBLK, axis=2)
    scaled = key_vectors * DK ** (-0.5)
    refreshed_cell = (
        keep[:, :, :, None] * cell_state
        + (admit * scaled)[:, :, :, None] * token_value_vectors[:, :, None, :]
    )
    new_normal = keep * normalizer + admit * scaled
    local_top = jnp.max(fresh, axis=2)
    weight_matrix = jnp.repeat(jnp.exp(fresh - local_top[:, :, None]), RBLK, axis=2) * queries
    numerator = jnp.einsum(
        "bhkv,bhk->bhv", refreshed_cell, weight_matrix, precision=lax.Precision.HIGHEST
    )
    denom = jnp.sum(new_normal * weight_matrix, axis=2)
    top, numerator, denom = combined_by_axis((local_top, numerator, denom), ROW, combine_pairs)
    readout = numerator / jnp.maximum(jnp.abs(denom), jnp.exp(-top))[:, :, None]
    running_totals, squares = together(
        (jnp.sum(readout, axis=2), jnp.sum(readout * readout, axis=2)), "col"
    )
    mean = running_totals / DV
    var = squares / DV - mean * mean
    normed = (readout - mean[:, :, None]) * lax.rsqrt(var + 1e-06)[:, :, None]
    gated = (normed * norm_gain * jax.nn.sigmoid(output_gate_logits)).astype(jnp.bfloat16)
    seq_rows = gated.shape[0]
    out_cols = out_weight.shape[2]
    partial_value = jnp.dot(
        gated.reshape(seq_rows, -1),
        lax.all_gather(out_weight, "hb", axis=0, tiled=True).reshape(-1, out_cols),
        preferred_element_type=jnp.float32,
    )
    layer_out = over_copies(partial_value, "col")
    return (layer_out, readout, refreshed_cell, new_normal, fresh)


def solution(mesh):
    torus = Mesh(
        mesh.devices.reshape(mesh.shape["hb"], 8, 2, mesh.shape["col"]),
        ("hb", "row_0", "row_1", "col"),
    )
    in_specs = (
        P("hb", None, ROW, "col"),
        P("hb", None, ROW),
        P("hb", None, ROW),
        P("hb", None, ROW),
        P("hb", None, ROW),
        P("hb", None, "col"),
        P("hb", None),
        P("hb", None),
        P("hb", None, "col"),
        P(None, "col"),
        P("hb", "col", ROW),
    )
    out_specs = (
        P("hb", ROW),
        P("hb", None, "col"),
        P("hb", None, ROW, "col"),
        P("hb", None, ROW),
        P("hb", None, ROW),
    )
    return jax.shard_map(local, mesh=torus, in_specs=in_specs, out_specs=out_specs, check_vma=False)
```

profile of v0, /device:TPU:1, one launch (start us, length us, event | category | flops | bytes accessed | tf_op | source)
XLA Modules:
  0.0 107.4 jit_solution(9087296757668042198)
XLA Ops:
  7.2 0.7 fusion.24
  7.9 0.7 subtract_exponential_fusion.2
  8.7 0.7 exponential_multiply_fusion
  9.5 1.6 %multiply_reduce_fusion.1 = (f32[64,8]{0,1:T(8,128)S(1)}, f32[64,8,16]{0,2,1:T(8,128)}, f32[64,8,16]{0,2,1:T(8,128)S(1)}, f32[64,8,16,1]{0,2,1,3:T(8,128)S(1)}) fusion(f32[64,8,16]{0,2,1:T(8,128)} %param.14, f32[64,8]{0,1:T(8,128)S(1)} %bitcast.431, f32[64,8,16]{0,2,1:T(8,128)} %param.12, f32[64,8]{0,1:T(8,128)S(1)} %bitcast.426, f32[64,8,16]{0,2,1:T(8,128)} %param.15, ...), kind=kLoop, calls=%fused_computation.41 | loop fusion | flops 48640 | bytes 204800 | tf_op jit(solution)/shard_map/reduce_sum | solution.py:94
  11.6 4.0 %multiply_add_fusion = f32[64,8,16,128]{3,2,1,0:T(8,128)S(1)} fusion(f32[64,8,16,128]{3,2,1,0:T(8,128)} %param.11, f32[64,8,128]{2,1,0:T(8,128)} %param.16, f32[64,8,16]{2,1,0:T(8,128)S(1)} %copy.34, f32[64,8]{1,0:T(8,128)S(1)} %copy.33), kind=kLoop, calls=%fused_computation | loop fusion | flops 3145728 | bytes 8685568 | tf_op jit(solution)/shard_map/add | solution.py:85
  15.7 2.0 %copy-done = f32[64,8,16,128]{3,2,1,0:T(8,128)} copy-done((f32[64,8,16,128]{3,2,1,0:T(8,128)}, f32[64,8,16,128]{3,2,1,0:T(8,128)S(1)}, u32[]{:S(2)}) %copy-start) | copy-done | bytes 4194328
  17.7 4.0 %fusion.81 = f32[64,8,1,128]{3,2,1,0:T(1,128)S(1)} fusion(f32[64,8,16,128]{3,2,1,0:T(8,128)S(1)} %multiply_add_fusion, f32[64,8,16,1]{2,3,1,0:T(1,128)S(1)} %copy.39), kind=kOutput, calls=%fused_computation.160 | convolution fusion | flops 12582912 | bytes 4489216 | tf_op jit(solution)/shard_map/bhkv,bhk->bhv/dot_general | solution.py:91
  21.7 0.7 pad_maximum_fusion
  22.5 12.6 %all_gather.19 = bf16[8,128,256]{2,1,0:T(8,128)(2,1)S(1)} all-gather(bf16[2,128,256]{2,1,0:T(8,128)(2,1)S(1)} %copy-done.2), channel_id=1, replica_groups=mesh['hb'=4,'row_0'=8,'row_1'=2,'col'=4] {'hb'}, dimensions={0}, use_global_device_ids=true | all-gather | bytes 655360 | tf_op jit(solution)/shard_map/all_gather | solution.py:108
  35.1 27.9 %all-gather.4.cloned.1.call-done = f32[4160,128]{1,0:T(8,128)} async-done(((f32[520,128]{1,0:T(8,128)}), f32[4160,128]{1,0:T(8,128)}) %all-gather.4.cloned.1.call-update) | async-done | bytes 2129936 | tf_op jit(solution)/shard_map/all_gather | solution.py:21
  63.0 0.7 fusion.67
  63.7 0.8 fusion.28
  64.5 0.7 fusion.66
  65.2 0.7 fusion.64
  65.9 0.7 fusion.62
  66.6 2.5 %fusion.1 = f32[512,128]{1,0:T(8,128)S(1)} fusion(f32[8,520,128]{2,1,0:T(8,128)} %bitcast.423, f32[512]{0:T(512)S(1)} %get-tuple-element.37, f32[512]{0:T(512)S(1)} %get-tuple-element.34, f32[512]{0:T(512)S(1)} %get-tuple-element.36, f32[512]{0:T(512)S(1)} %get-tuple-element.35, f32[512]{0:T(512)S(1)} %get-tuple-element.33, f32[512]{0:T(512)S(1)} %get-tuple-element.31, ...), kind=kLoop, calls=%fused_computation.6 | loop fusion | flops 1376256 | bytes 2387968 | tf_op jit(solution)/shard_map/add | solution.py:61
  69.1 7.4 %all-gather.1 = f32[1040,128]{1,0:T(8,128)S(1)} all-gather(f32[520,128]{1,0:T(8,128)S(1)} %pad_maximum_fusion.1), channel_id=3, replica_groups=mesh['hb'=4,'row_0'=8,'row_1'=2,'col'=4] {'row_1'}, dimensions={0}, use_global_device_ids=true | all-gather | bytes 798720 | tf_op jit(solution)/shard_map/all_gather | solution.py:21
  76.6 0.4 fusion.78
  77.0 0.6 broadcast_in_dim.10
  77.6 9.4 %all-to-all-start = ((f32[4,1,1024]{2,1,0:T(1,128)}), f32[4,1,1024]{2,1,0:T(1,128)S(1)}, u32[]{:S(2)}, u32[]{:S(2)}) async-start(f32[4,1,1024]{2,1,0:T(1,128)} %broadcast_in_dim.10), calls=%async_computation | async-start | bytes 32768 | tf_op jit(solution)/shard_map/all_to_all | solution.py:41
  87.4 2.8 %all-to-all-done = f32[4,1,1024]{2,1,0:T(1,128)S(1)} async-done(((f32[4,1,1024]{2,1,0:T(1,128)}), f32[4,1,1024]{2,1,0:T(1,128)S(1)}, u32[]{:S(2)}, u32[]{:S(2)}) %all-to-all-start) | async-done | bytes 16416 | tf_op jit(solution)/shard_map/all_to_all | solution.py:41
  90.4 1.1 %multiply_convert_fusion = (bf16[64,8,128]{2,1,0:T(8,128)(2,1)S(1)}, f32[64,8,128]{2,1,0:T(8,128)}) fusion(f32[64,8,128]{2,1,0:T(8,128)S(1)} %copy-done.1, f32[8,128]{1,0:T(8,128)S(1)} %copy-done.4, f32[64,8]{1,0:T(8,128)S(1)} %get-tuple-element.53, f32[64,8]{1,0:T(8,128)S(1)} %div.32, f32[64,8]{1,0:T(8,128)S(1)} %get-tuple-element.47, ...), kind=kLoop, calls=%fused_computation.37 | loop fusion | flops 786432 | bytes 1193984 | tf_op jit(solution)/shard_map/convert_element_type | solution.py:103
  91.8 8.1 %all_to_all.11 = f32[4,64,256]{2,1,0:T(8,128)S(1)} all-to-all(f32[4,64,256]{2,1,0:T(8,128)S(1)} %broadcast_in_dim.11), channel_id=1, replica_groups=mesh['hb'=4,'row_0'=8,'row_1'=2,'col'=4] {'col'}, dimensions={0} | all-to-all | bytes 524288 | tf_op jit(solution)/shard_map/all_to_all | solution.py:41
  99.9 0.6 reduce_sum.49
  (33 shorter events, 1.6 us)
Async XLA Ops:
  7.2 55.8 %all-gather.4.cloned.1.call-start = ((), (), s32[]{:S(2)}) async-start(), calls=%async_computation.2 | async-start | bytes 2396160 | tf_op jit(solution)/shard_map/all_gather | solution.py:21
  8.6 7.0 %copy-start.3 = (f32[64,1,8]{0,2,1:T(8,128)}, f32[64,1,8]{0,2,1:T(8,128)S(1)}, u32[]{:S(2)}) copy-start(f32[64,1,8]{0,2,1:T(8,128)S(1)} %get-tuple-element.55) | copy-start | bytes 6148
  15.7 2.0 %copy-start = (f32[64,8,16,128]{3,2,1,0:T(8,128)}, f32[64,8,16,128]{3,2,1,0:T(8,128)S(1)}, u32[]{:S(2)}) copy-start(f32[64,8,16,128]{3,2,1,0:T(8,128)S(1)} %multiply_add_fusion) | copy-start | bytes 12582916
  17.7 4.8 %copy-start.2 = (bf16[2,128,256]{2,1,0:T(8,128)(2,1)S(1)}, bf16[2,128,256]{2,1,0:T(8,128)(2,1)}, u32[]{:S(2)}) copy-start(bf16[2,128,256]{2,1,0:T(8,128)(2,1)} %param.21) | copy-start | bytes 393220
  21.7 68.7 %copy-start.1 = (f32[64,8,128]{2,1,0:T(8,128)S(1)}, f32[64,8,128]{2,1,0:T(8,128)}, u32[]{:S(2)}) copy-start(f32[64,8,128]{2,1,0:T(8,128)} %param.19) | copy-start | bytes 786436
  21.7 68.7 %copy-start.4 = (f32[8,128]{1,0:T(8,128)S(1)}, f32[8,128]{1,0:T(8,128)}, u32[]{:S(2)}) copy-start(f32[8,128]{1,0:T(8,128)} %param.20) | copy-start | bytes 12292
  77.6 12.5 %all-to-all-start = ((f32[4,1,1024]{2,1,0:T(1,128)}), f32[4,1,1024]{2,1,0:T(1,128)S(1)}, u32[]{:S(2)}, u32[]{:S(2)}) async-start(f32[4,1,1024]{2,1,0:T(1,128)} %broadcast_in_dim.10), calls=%async_computation | async-start | bytes 32768 | tf_op jit(solution)/shard_map/all_to_all | solution.py:41
Sparse Core Ops, SparseCore 0:
  22.6 40.3 all-gather.3
where the time goes:
time: 108 us; the launch traced here: 107 us
  waiting for transfers between devices  30.7 us (28%)
  blocking collectives  28.1 us (26%)
  other arithmetic  16.8 us (16%)
  between operations  14.2 us (13%)
  starting transfers between devices  9.42 us (9%)
  matrix products  4.21 us (4%)
  local copies, waits for them, and re-layouts  3.9 us (4%)
    all_gather x1, waiting for transfers between devices, all_in_one(): both, at, found = (lax.all_gather(jnp.concatenate(lines), axis), 0, {})  27.9 us
    all_gather x1, blocking collectives, local(): lax.all_gather(out_weight, 'hb', axis=0, tiled=True).reshape(-1, out_cols)  12.6 us
    all_to_all x1, starting transfers between devices, sent_to_all(): return lax.all_to_all(copies, axis, split_axis=0, concat_axis=0, tiled=True)  9.38 us
    all_to_all x1, blocking collectives, sent_to_all(): return lax.all_to_all(copies, axis, split_axis=0, concat_axis=0, tiled=True)  8.09 us
    all_gather x1, blocking collectives, all_in_one(): both, at, found = (lax.all_gather(jnp.concatenate(lines), axis), 0, {})  7.44 us
    add x1, other arithmetic, local(): keep[:, :, :, None] * cell_state  4.01 us
    dot_general x1, matrix products, local(): jnp.einsum('bhkv,bhk->bhv', refreshed_cell, weight_matrix, precision=lax....  4.01 us
    all_to_all x1, waiting for transfers between devices, sent_to_all(): return lax.all_to_all(copies, axis, split_axis=0, concat_axis=0, tiled=True)  2.76 us
  transfers between devices with their start and end apart: 2, of which 2 were waited for; matrix products, arithmetic and copies ran while one was open for 0% of the time, Pallas kernels for 0%

commit v1 on v0

--- a/solution.py
+++ b/solution.py
@@ -3,6 +3,7 @@
 from jax import lax
 from jax.sharding import Mesh
 from jax.sharding import PartitionSpec as P
+from jax.lax import all_to_all, axis_size
 
 DK = 256
 DV = 512
@@ -103,9 +104,15 @@
     gated = (normed * norm_gain * jax.nn.sigmoid(output_gate_logits)).astype(jnp.bfloat16)
     seq_rows = gated.shape[0]
     out_cols = out_weight.shape[2]
+
+    def edge_open(vals):
+        base_arr = axis_size("hb")
+        piece_out = jnp.concatenate([vals] * base_arr, axis=0)
+        return all_to_all(piece_out, "hb", 0, 0, tiled=True)
+
     partial_value = jnp.dot(
         gated.reshape(seq_rows, -1),
-        lax.all_gather(out_weight, "hb", axis=0, tiled=True).reshape(-1, out_cols),
+        edge_open(out_weight).reshape(-1, out_cols),
         preferred_element_type=jnp.float32,
     )
     layer_out = over_copies(partial_value, "col")

time: 108 us -> 120 us (1.11)
  waiting for transfers between devices: 30.7 us -> 49.3 us
  blocking collectives: 28.1 us -> 17 us
  starting transfers between devices: 9.42 us -> 13.4 us
    all_gather x1 -> x0, blocking collectives: 12.6 us -> none  [local(): lax.all_gather(out_weight, 'hb', axis=0, tiled=True).reshape(-1, out_cols)]
    all_gather x1, waiting for transfers between devices: 27.9 us -> 39.7 us  [all_in_one(): both, at, found = (lax.all_gather(jnp.concatenate(lines), axis), 0, {})]
    all_to_all x0 -> x1, waiting for transfers between devices: none -> 6.89 us  [edge_open(): return all_to_all(piece_out, 'hb', 0, 0, tiled=True)]
    all_to_all x0 -> x1, starting transfers between devices: none -> 4 us  [edge_open(): return all_to_all(piece_out, 'hb', 0, 0, tiled=True)]
    all_to_all x1, blocking collectives: 8.09 us -> 9.52 us  [sent_to_all(): return lax.all_to_all(copies, axis, split_axis=0, concat_axis=0, tiled=True)]
  transfers between devices with their start and end apart: 2 -> 3, of which waited for: 2 -> 3; matrix products, arithmetic and copies ran while one was open for 0% -> 2% of each run, Pallas kernels for 0% -> 0%
where the time goes in v1:
time: 120 us
  waiting for transfers between devices  49.3 us (41%)
  other arithmetic  17.6 us (15%)
  blocking collectives  17 us (14%)
  between operations  14.2 us (12%)
  starting transfers between devices  13.4 us (11%)
  matrix products  4.21 us (4%)
  local copies, waits for them, and re-layouts  3.9 us (3%)
    all_gather x1, waiting for transfers between devices, all_in_one(): both, at, found = (lax.all_gather(jnp.concatenate(lines), axis), 0, {})  39.7 us
    all_to_all x1, blocking collectives, sent_to_all(): return lax.all_to_all(copies, axis, split_axis=0, concat_axis=0, tiled=True)  9.52 us
    all_to_all x1, starting transfers between devices, sent_to_all(): return lax.all_to_all(copies, axis, split_axis=0, concat_axis=0, tiled=True)  9.38 us
    all_gather x1, blocking collectives, all_in_one(): both, at, found = (lax.all_gather(jnp.concatenate(lines), axis), 0, {})  7.44 us
    all_to_all x1, waiting for transfers between devices, edge_open(): return all_to_all(piece_out, 'hb', 0, 0, tiled=True)  6.89 us
    add x1, other arithmetic, local(): keep[:, :, :, None] * cell_state  4.01 us
    dot_general x1, matrix products, local(): jnp.einsum('bhkv,bhk->bhv', refreshed_cell, weight_matrix, precision=lax....  4.01 us
    all_to_all x1, starting transfers between devices, edge_open(): return all_to_all(piece_out, 'hb', 0, 0, tiled=True)  4 us
  transfers between devices with their start and end apart: 3, of which 3 were waited for; matrix products, arithmetic and copies ran while one was open for 2% of the time, Pallas kernels for 0%

profile of v1, /device:TPU:1, one launch (start us, length us, event | category | flops | bytes accessed | tf_op | source)
XLA Modules:
  0.0 119.7 jit_solution(4297350612831598413)
XLA Ops:
  7.2 0.7 fusion.24
  7.9 0.7 subtract_exponential_fusion.2
  8.7 0.7 exponential_multiply_fusion
  9.5 1.6 %multiply_reduce_fusion.1 = (f32[64,8]{0,1:T(8,128)S(1)}, f32[64,8,16]{0,2,1:T(8,128)}, f32[64,8,16]{0,2,1:T(8,128)S(1)}, f32[64,8,16,1]{0,2,1,3:T(8,128)S(1)}) fusion(f32[64,8,16]{0,2,1:T(8,128)} %param.14, f32[64,8]{0,1:T(8,128)S(1)} %bitcast.431, f32[64,8,16]{0,2,1:T(8,128)} %param.12, f32[64,8]{0,1:T(8,128)S(1)} %bitcast.426, f32[64,8,16]{0,2,1:T(8,128)} %param.15, ...), kind=kLoop, calls=%fused_computation.42 | loop fusion | flops 48640 | bytes 204800 | tf_op jit(solution)/shard_map/reduce_sum | solution.py:95
  11.6 4.0 %multiply_add_fusion = f32[64,8,16,128]{3,2,1,0:T(8,128)S(1)} fusion(f32[64,8,16,128]{3,2,1,0:T(8,128)} %param.11, f32[64,8,128]{2,1,0:T(8,128)} %param.16, f32[64,8,16]{2,1,0:T(8,128)S(1)} %copy.34, f32[64,8]{1,0:T(8,128)S(1)} %copy.33), kind=kLoop, calls=%fused_computation | loop fusion | flops 3145728 | bytes 8685568 | tf_op jit(solution)/shard_map/add | solution.py:86
  15.7 2.0 %copy-done = f32[64,8,16,128]{3,2,1,0:T(8,128)} copy-done((f32[64,8,16,128]{3,2,1,0:T(8,128)}, f32[64,8,16,128]{3,2,1,0:T(8,128)S(1)}, u32[]{:S(2)}) %copy-start) | copy-done | bytes 4194328
  17.7 4.0 %fusion.81 = f32[64,8,1,128]{3,2,1,0:T(1,128)S(1)} fusion(f32[64,8,16,128]{3,2,1,0:T(8,128)S(1)} %multiply_add_fusion, f32[64,8,16,1]{2,3,1,0:T(1,128)S(1)} %copy.39), kind=kOutput, calls=%fused_computation.161 | convolution fusion | flops 12582912 | bytes 4489216 | tf_op jit(solution)/shard_map/bhkv,bhk->bhv/dot_general | solution.py:92
  21.7 0.7 pad_maximum_fusion.1
  22.5 0.8 pad_maximum_fusion
  23.3 39.7 %all-gather.4.cloned.1.call-done = f32[4160,128]{1,0:T(8,128)} async-done(((f32[520,128]{1,0:T(8,128)}), f32[4160,128]{1,0:T(8,128)}) %all-gather.4.cloned.1.call-update) | async-done | bytes 2129936 | tf_op jit(solution)/shard_map/all_gather | solution.py:22
  63.0 0.7 fusion.67
  63.7 0.8 fusion.28
  64.5 0.7 fusion.66
  65.2 0.7 fusion.64
  65.9 0.7 fusion.62
  66.6 2.5 %fusion.1 = f32[512,128]{1,0:T(8,128)S(1)} fusion(f32[8,520,128]{2,1,0:T(8,128)} %bitcast.423, f32[512]{0:T(512)S(1)} %get-tuple-element.37, f32[512]{0:T(512)S(1)} %get-tuple-element.34, f32[512]{0:T(512)S(1)} %get-tuple-element.36, f32[512]{0:T(512)S(1)} %get-tuple-element.35, f32[512]{0:T(512)S(1)} %get-tuple-element.33, f32[512]{0:T(512)S(1)} %get-tuple-element.31, ...), kind=kLoop, calls=%fused_computation.7 | loop fusion | flops 1376256 | bytes 2387968 | tf_op jit(solution)/shard_map/add | solution.py:62
  69.1 7.4 %all-gather.1 = f32[1040,128]{1,0:T(8,128)S(1)} all-gather(f32[520,128]{1,0:T(8,128)S(1)} %pad_maximum_fusion.2), channel_id=3, replica_groups=mesh['hb'=4,'row_0'=8,'row_1'=2,'col'=4] {'row_1'}, dimensions={0}, use_global_device_ids=true | all-gather | bytes 798720 | tf_op jit(solution)/shard_map/all_gather | solution.py:22
  77.6 9.4 %all-to-all-start = ((f32[4,1,1024]{2,1,0:T(1,128)}), f32[4,1,1024]{2,1,0:T(1,128)S(1)}, u32[]{:S(2)}, u32[]{:S(2)}) async-start(f32[4,1,1024]{2,1,0:T(1,128)} %broadcast_in_dim.10), calls=%async_computation | async-start | bytes 32768 | tf_op jit(solution)/shard_map/all_to_all | solution.py:42
  87.4 2.8 %all-to-all-done = f32[4,1,1024]{2,1,0:T(1,128)S(1)} async-done(((f32[4,1,1024]{2,1,0:T(1,128)}), f32[4,1,1024]{2,1,0:T(1,128)S(1)}, u32[]{:S(2)}, u32[]{:S(2)}) %all-to-all-start) | async-done | bytes 16416 | tf_op jit(solution)/shard_map/all_to_all | solution.py:42
  90.2 4.0 %all-to-all-start.1 = ((bf16[8,128,256]{2,1,0:T(8,128)(2,1)}), bf16[8,128,256]{2,1,0:T(8,128)(2,1)S(1)}, u32[]{:S(2)}, u32[]{:S(2)}) async-start(bf16[8,128,256]{2,1,0:T(8,128)(2,1)} %pad_maximum_fusion), calls=%async_computation.1 | async-start | bytes 1048576 | tf_op jit(solution)/shard_map/all_to_all | solution.py:111
  94.4 1.1 multiply_convert_fusion
  95.5 6.9 %all-to-all-done.1 = bf16[8,128,256]{2,1,0:T(8,128)(2,1)S(1)} async-done(((bf16[8,128,256]{2,1,0:T(8,128)(2,1)}), bf16[8,128,256]{2,1,0:T(8,128)(2,1)S(1)}, u32[]{:S(2)}, u32[]{:S(2)}) %all-to-all-start.1) | async-done | bytes 524320 | tf_op jit(solution)/shard_map/all_to_all | solution.py:111
  102.7 9.5 %all_to_all.16 = f32[4,64,256]{2,1,0:T(8,128)S(1)} all-to-all(f32[4,64,256]{2,1,0:T(8,128)S(1)} %broadcast_in_dim.11), channel_id=1, replica_groups=mesh['hb'=4,'row_0'=8,'row_1'=2,'col'=4] {'col'}, dimensions={0} | all-to-all | bytes 524288 | tf_op jit(solution)/shard_map/all_to_all | solution.py:42
  112.2 0.6 reduce_sum.49
  (35 shorter events, 2.7 us)
Async XLA Ops:
  7.2 55.8 %all-gather.4.cloned.1.call-start = ((), (), s32[]{:S(2)}) async-start(), calls=%async_computation.3 | async-start | bytes 2396160 | tf_op jit(solution)/shard_map/all_gather | solution.py:22
  8.6 7.0 %copy-start.3 = (f32[64,1,8]{0,2,1:T(8,128)}, f32[64,1,8]{0,2,1:T(8,128)S(1)}, u32[]{:S(2)}) copy-start(f32[64,1,8]{0,2,1:T(8,128)S(1)} %get-tuple-element.55) | copy-start | bytes 6148
  15.7 2.0 %copy-start = (f32[64,8,16,128]{3,2,1,0:T(8,128)}, f32[64,8,16,128]{3,2,1,0:T(8,128)S(1)}, u32[]{:S(2)}) copy-start(f32[64,8,16,128]{3,2,1,0:T(8,128)S(1)} %multiply_add_fusion) | copy-start | bytes 12582916
  17.7 4.8 %copy-start.2 = (bf16[2,128,256]{2,1,0:T(8,128)(2,1)S(1)}, bf16[2,128,256]{2,1,0:T(8,128)(2,1)}, u32[]{:S(2)}) copy-start(bf16[2,128,256]{2,1,0:T(8,128)(2,1)} %param.21) | copy-start | bytes 393220
  21.7 72.7 %copy-start.1 = (f32[64,8,128]{2,1,0:T(8,128)S(1)}, f32[64,8,128]{2,1,0:T(8,128)}, u32[]{:S(2)}) copy-start(f32[64,8,128]{2,1,0:T(8,128)} %param.19) | copy-start | bytes 786436
  21.7 72.7 %copy-start.4 = (f32[8,128]{1,0:T(8,128)S(1)}, f32[8,128]{1,0:T(8,128)}, u32[]{:S(2)}) copy-start(f32[8,128]{1,0:T(8,128)} %param.20) | copy-start | bytes 12292
  77.6 12.5 %all-to-all-start = ((f32[4,1,1024]{2,1,0:T(1,128)}), f32[4,1,1024]{2,1,0:T(1,128)S(1)}, u32[]{:S(2)}, u32[]{:S(2)}) async-start(f32[4,1,1024]{2,1,0:T(1,128)} %broadcast_in_dim.10), calls=%async_computation | async-start | bytes 32768 | tf_op jit(solution)/shard_map/all_to_all | solution.py:42
  90.2 12.3 %all-to-all-start.1 = ((bf16[8,128,256]{2,1,0:T(8,128)(2,1)}), bf16[8,128,256]{2,1,0:T(8,128)(2,1)S(1)}, u32[]{:S(2)}, u32[]{:S(2)}) async-start(bf16[8,128,256]{2,1,0:T(8,128)(2,1)} %pad_maximum_fusion), calls=%async_computation.1 | async-start | bytes 1048576 | tf_op jit(solution)/shard_map/all_to_all | solution.py:111
Sparse Core Ops, SparseCore 0:
  22.6 40.3 all-gather.3
